TPU v7x, 32 devices: a whole 2x2x4 slice. The times are simulated.
32 devices in a mesh: dp: 8 (over z, y), sub: 4 (over x, core).
Axes of the slice: x: 2, y: 2, z: 4, core: 2. Of those that a mesh axis runs over, the one named last changes fastest.
Arguments:
- queries: bfloat16 [32, 64, 576], P('dp'), may hold values from -195 to 195
- own_cache: bfloat16 [32, 1024, 576], P('dp', 'sub'), may hold values from -8 to 8
- own_len: int32 [32, 4], P('dp', 'sub'), may hold values from 2 to 256
- host_cache: bfloat16 [8, 4, 8, 1024, 576], P('dp', 'sub'), may hold values from -8 to 8
- host_len: int32 [8, 4, 8], P('dp', 'sub'), may hold values from 2 to 1024
- page_plan: int32 [8, 4, 8], P('dp', 'sub'), may hold values from 0 to 3
- value_up: bfloat16 [64, 512, 128], P('sub'), may hold values from -0.25 to 0.25
Outputs:
- attended: bfloat16 [32, 64, 128], P('dp', 'sub')
All inputs are finite; a program needn't handle non-finite values.
Results may differ from a plain program's by a relative error of at most 0.008.
Values may be sent and summed in bfloat16 or wider, within the bound.
No kernel may reach another device: no remote copies, remote signals or barrier semaphores. Data moves between devices by JAX's collectives and lax.ppermute only.
A program may use at most 128 MiB of HBM per device.

v0:
```python
import jax
import jax.numpy as jnp
from jax import lax
from jax.sharding import PartitionSpec as P

DL = 512
score_scale = 192 ** (-0.5)
masked_score = -1e30


def attend(queries, slot_cache, lengths):
    scores = (
        jnp.einsum("phd,ptd->pht", queries, slot_cache, preferred_element_type=jnp.float32)
        * score_scale
    )
    position = lax.broadcasted_iota(jnp.int32, (1, 1, slot_cache.shape[1]), 2)
    scores = jnp.where(position < lengths[:, None, None], scores, masked_score)
    largest = jnp.max(scores, axis=2, keepdims=True)
    exponent = jnp.exp(scores - largest)
    totals = jnp.sum(exponent, axis=2)
    weights = exponent.astype(jnp.bfloat16)
    weighted = jnp.einsum(
        "pht,ptd->phd", weights, slot_cache[:, :, :DL], preferred_element_type=jnp.float32
    )
    return (weighted / totals[:, :, None], largest[:, :, 0] + jnp.log(totals))


def combine_group(device_out, device_lse):
    pieces_out, pieces_lse = (
        lax.all_to_all(device_out[None], "sub", split_axis=2, concat_axis=0, tiled=True),
        lax.all_to_all(device_lse[None], "sub", split_axis=2, concat_axis=0, tiled=True),
    )
    piece_peak = jnp.max(pieces_lse, axis=0)
    piece_weight = jnp.exp(pieces_lse - piece_peak[None])
    weight_total = jnp.sum(piece_weight, axis=0)
    share_out = jnp.sum(piece_weight[..., None] * pieces_out, axis=0) / weight_total[..., None]
    share_lse = piece_peak + jnp.log(weight_total)
    return (share_out, share_lse)


def local(queries, own_cache, own_len, host_cache, host_len, page_plan, value_up):
    groups = lax.axis_size("dp")
    request_count, head_count, width = queries.shape
    targets = page_plan.reshape(groups)
    matched = targets[:, None] == lax.broadcasted_iota(jnp.int32, (groups, request_count), 1)
    onehot_table = matched.astype(jnp.bfloat16)
    outgoing = jnp.dot(
        onehot_table,
        queries.reshape(request_count, head_count * width),
        preferred_element_type=jnp.float32,
    )
    outgoing = outgoing.astype(jnp.bfloat16).reshape(groups, head_count, width)
    slot_cache = host_cache.reshape(groups, host_cache.shape[3], width)
    slot_lengths = host_len.reshape(groups)
    helper_out, helper_lse = attend(
        lax.all_to_all(outgoing, "dp", split_axis=0, concat_axis=0, tiled=True),
        slot_cache,
        slot_lengths,
    )
    back_out = lax.all_to_all(helper_out, "dp", split_axis=0, concat_axis=0, tiled=True)
    back_lse = lax.all_to_all(helper_lse, "dp", split_axis=0, concat_axis=0, tiled=True)
    own_out, own_lse = attend(queries, own_cache, own_len.reshape(request_count))
    masked = jnp.where(matched[:, :, None], back_lse[:, None, :], masked_score)
    largest = jnp.maximum(own_lse, jnp.max(masked, axis=0))
    own_weight = jnp.exp(own_lse - largest)
    help_weight = jnp.exp(masked - largest[None])
    gathered = jnp.einsum("pch,phd->chd", help_weight, back_out, precision=lax.Precision.HIGHEST)
    totals = own_weight + jnp.sum(help_weight, axis=0)
    device_out = (own_weight[..., None] * own_out + gathered) / totals[..., None]
    device_lse = largest + jnp.log(totals)
    latent, unused_lse = combine_group(device_out, device_lse)
    latent = latent.astype(jnp.bfloat16)
    result = jnp.einsum("chd,hde->che", latent, value_up, preferred_element_type=jnp.float32)
    return result.astype(jnp.bfloat16)


def solution(mesh):
    return jax.shard_map(
        local,
        mesh=mesh,
        in_specs=(
            P("dp", None, None),
            P("dp", "sub", None),
            P("dp", "sub"),
            P("dp", "sub", None, None, None),
            P("dp", "sub", None),
            P("dp", "sub", None),
            P("sub", None, None),
        ),
        out_specs=P("dp", "sub", None),
        check_vma=False,
    )
```

profile of v0, /device:TPU:0, one launch (start us, length us, event | category | flops | bytes accessed | tf_op | source)
XLA Modules:
  0.0 100.5 jit_solution(15990378591862014049)
XLA Ops:
  0.0 0.0 copy-start
  0.0 1.5 %reshape.178 = bf16[4,36864]{1,0:T(4,128)(2,1)S(1)} reshape(bf16[4,64,576]{2,1,0:T(8,128)(2,1)} %param.7) | data formatting | bytes 589824 | tf_op jit(solution)/shard_map/reshape | solution.py:49
  1.5 1.0 %convolution_convert_fusion = bf16[8,36864]{1,0:T(8,128)(2,1)S(1)} fusion(bf16[4,36864]{1,0:T(4,128)(2,1)S(1)} %reshape.178, s32[8]{0:T(128)} %bitcast.61), kind=kOutput, calls=%fused_computation | convolution fusion | flops 2654240 | bytes 884768 | tf_op jit(solution)/shard_map/dot_general | solution.py:47
  2.6 1.7 %reshape.179 = bf16[8,64,576]{2,1,0:T(8,128)(2,1)} reshape(bf16[8,36864]{1,0:T(8,128)(2,1)S(1)} %convolution_convert_fusion) | data formatting | bytes 1179648 | tf_op jit(solution)/shard_map/reshape | solution.py:52
  4.2 7.3 %all-to-all-start = ((bf16[8,64,576]{2,1,0:T(8,128)(2,1)}), bf16[8,64,576]{2,1,0:T(8,128)(2,1)S(1)}, u32[]{:S(2)}, u32[]{:S(2)}) async-start(bf16[8,64,576]{2,1,0:T(8,128)(2,1)} %reshape.179), calls=%async_computation | async-start | bytes 1310720 | tf_op jit(solution)/shard_map/all_to_all | solution.py:56
  11.5 0.0 copy-start.5
  11.5 14.1 %copy.28 = bf16[1,1,8,1024,576]{4,3,2,1,0:T(8,128)(2,1)} copy(bf16[1,1,8,1024,576]{3,4,2,1,0:T(8,128)(2,1)} %param.10) | data formatting | bytes 18874368 | tf_op args[3]
  25.7 0.0 copy-done.5
  25.7 0.1 iota_compare_fusion
  25.7 3.1 %all-to-all-done = bf16[8,64,576]{2,1,0:T(8,128)(2,1)S(1)} async-done(((bf16[8,64,576]{2,1,0:T(8,128)(2,1)}), bf16[8,64,576]{2,1,0:T(8,128)(2,1)S(1)}, u32[]{:S(2)}, u32[]{:S(2)}) %all-to-all-start) | async-done | bytes 589856 | tf_op jit(solution)/shard_map/all_to_all | solution.py:56
  28.8 5.7 %fusion.4 = (f32[8,64]{1,0:T(8,128)S(1)}, f32[8,64,1024]{2,1,0:T(8,128)S(1)}) fusion(pred[8,1024]{1,0:T(8,128)(4,1)S(1)} %iota_compare_fusion, bf16[8,64,576]{2,1,0:T(8,128)(2,1)S(1)} %all-to-all-done, bf16[1,1,8,1024,576]{3,4,2,1,0:T(8,128)(2,1)} %param.10), kind=kOutput, calls=%fused_computation.7 | convolution fusion | flops 605552128 | bytes 12134400 | tf_op jit(solution)/shard_map/phd,ptd->pht/dot_general | solution.py:13
  34.5 0.0 copy-start.1
  34.5 1.3 %copy-done.1 = f32[8,64,1024]{2,1,0:T(8,128)} copy-done((f32[8,64,1024]{2,1,0:T(8,128)}, f32[8,64,1024]{2,1,0:T(8,128)S(1)}, u32[]{:S(2)}) %copy-start.1) | copy-done | bytes 2097176
  35.8 0.6 fusion.6
  36.4 0.6 log_add_fusion
  37.0 3.6 %all-to-all-start.1 = ((f32[8,1,64]{2,1,0:T(1,128)}), f32[8,1,64]{2,1,0:T(1,128)S(1)}, u32[]{:S(2)}, u32[]{:S(2)}) async-start(f32[8,1,64]{2,1,0:T(1,128)} %bitcast.6), calls=%async_computation.1 | async-start | bytes 8192 | tf_op jit(solution)/shard_map/all_to_all | solution.py:61
  40.6 6.7 %fusion.21 = f32[8,64,512]{2,1,0:T(8,128)} fusion(bf16[8,1024,576]{2,1,0:T(8,128)(2,1)} %bitcast.57, f32[8,64,1024]{2,1,0:T(8,128)} %copy-done.1, f32[8,64]{1,0:T(8,128)S(1)} %get-tuple-element.9, pred[8,1024]{1,0:T(8,128)(4,1)S(1)} %iota_compare_fusion, f32[8,64]{1,0:T(8,128)S(1)} %fusion.6), kind=kOutput, calls=%fused_computation.26 | convolution fusion | flops 539230208 | bytes 11546624 | tf_op jit(solution)/shard_map/pht,ptd->phd/dot_general | solution.py:22
  47.3 0.0 all-to-all-done.1
  47.3 6.1 %all-to-all-start.3 = ((f32[8,64,512]{2,1,0:T(8,128)}), f32[8,64,512]{2,1,0:T(8,128)S(1)}, u32[]{:S(2)}, u32[]{:S(2)}) async-start(f32[8,64,512]{2,1,0:T(8,128)} %fusion.21), calls=%async_computation.3 | async-start | bytes 2097152 | tf_op jit(solution)/shard_map/all_to_all | solution.py:60
  53.5 0.0 copy-done.6
  53.5 0.1 iota_compare_fusion.1
  53.5 0.0 copy-done.2
  53.5 1.7 %fusion.50 = (f32[4,64]{1,0:T(4,128)S(1)}, f32[4,64,256]{2,1,0:T(8,128)S(1)}) fusion(bf16[4,64,576]{2,1,0:T(8,128)(2,1)S(1)} %copy-done.2, bf16[4,256,576]{1,2,0:T(8,128)(2,1)} %param.8, pred[4,256]{1,0:T(4,128)(4,1)S(1)} %iota_compare_fusion.1), kind=kOutput, calls=%fused_computation.64 | convolution fusion | flops 75693824 | bytes 1738752 | tf_op jit(solution)/shard_map/phd,ptd->pht/dot_general | solution.py:13
  55.3 0.0 copy-start.3
  55.3 0.7 copy-done.3
  55.9 0.2 fusion.28
  56.1 0.0 copy-done.4
  56.2 0.1 copy.30
  56.2 0.1 select_reduce_fusion
  56.4 0.1 copy.31
  56.5 0.1 copy.33
  56.6 0.2 fusion.31
  56.8 0.1 copy.34
  56.9 0.7 copy.35
  57.6 21.4 %all-to-all-done.3 = f32[8,64,512]{2,1,0:T(8,128)S(1)} async-done(((f32[8,64,512]{2,1,0:T(8,128)}), f32[8,64,512]{2,1,0:T(8,128)S(1)}, u32[]{:S(2)}, u32[]{:S(2)}) %all-to-all-start.3) | async-done | bytes 1048608 | tf_op jit(solution)/shard_map/all_to_all | solution.py:60
  79.0 3.3 %all-to-all-start.2 = ((f32[1,4,64]{1,0,2:T(1,128)}), f32[1,4,64]{1,0,2:T(1,128)S(1)}, u32[]{:S(2)}, u32[]{:S(2)}) async-start(f32[1,4,64]{1,0,2:T(1,128)} %copy.35), calls=%async_computation.2 | async-start | bytes 65536 | tf_op jit(solution)/shard_map/all_to_all | solution.py:31
  82.3 1.6 %fusion.14 = f32[64,512,4]{1,2,0:T(4,128)S(1)} fusion(f32[8,64,512]{2,1,0:T(8,128)S(1)} %all-to-all-done.3, f32[4,64]{0,1:T(8,128)S(1)} %copy.33, f32[8,64]{0,1:T(8,128)S(1)} %copy.30, pred[8,4]{0,1:T(4,128)(4,1)S(1)} %iota_compare_fusion.2), kind=kOutput, calls=%fused_computation.19 | convolution fusion | flops 12587008 | bytes 1575968 | tf_op jit(solution)/shard_map/pch,phd->chd/dot_general | solution.py:67
  83.9 1.8 %fusion.10 = f32[1,4,64,512]{3,2,1,0:T(8,128)S(1)} fusion(bf16[4,256,576]{1,2,0:T(8,128)(2,1)} %param.8, f32[64,512,4]{1,2,0:T(4,128)S(1)} %fusion.14, f32[4,64]{1,0:T(4,128)S(1)} %get-tuple-element.7, f32[4,64]{1,0:T(4,128)S(1)} %fusion.28, f32[4,64]{1,0:T(4,128)S(1)} %get-tuple-element.8, f32[4,64,256]{2,1,0:T(8,128)} %copy-done.3, ...), kind=kOutput, calls=%fused_computation.14 | convolution fusion | flops 67764224 | bytes 2363392 | tf_op jit(solution)/shard_map/pht,ptd->phd/dot_general | solution.py:22
  85.8 1.1 %copy.41 = f32[1,4,64,512]{3,1,0,2:T(4,128)} copy(f32[1,4,64,512]{3,2,1,0:T(8,128)S(1)} %fusion.10) | data formatting | bytes 1048576 | tf_op jit(solution)/shard_map/broadcast_in_dim | solution.py:30
  86.9 0.0 all-to-all-done.2
  86.9 3.5 %all-to-all-start.4 = ((f32[1,4,64,512]{3,1,0,2:T(4,128)}), f32[1,4,64,512]{3,1,0,2:T(4,128)S(1)}, u32[]{:S(2)}, u32[]{:S(2)}) async-start(f32[1,4,64,512]{3,1,0,2:T(4,128)} %copy.41), calls=%async_computation.4 | async-start | bytes 1048576 | tf_op jit(solution)/shard_map/all_to_all | solution.py:30
  90.4 0.1 copy.36
  90.5 8.6 %all-to-all-done.4 = f32[1,4,64,512]{3,1,0,2:T(4,128)S(1)} async-done(((f32[1,4,64,512]{3,1,0,2:T(4,128)}), f32[1,4,64,512]{3,1,0,2:T(4,128)S(1)}, u32[]{:S(2)}, u32[]{:S(2)}) %all-to-all-start.4) | async-done | bytes 524320 | tf_op jit(solution)/shard_map/all_to_all | solution.py:30
  99.2 0.2 fusion.26
  99.3 0.1 divide_convert_fusion
  99.4 0.0 copy-done
  99.4 0.4 fusion.12
  99.8 0.6 copy.44
  (9 shorter events, 0.1 us)
Async XLA Ops:
  0.0 99.4 %copy-start = (bf16[16,512,128]{2,1,0:T(8,128)(2,1)S(1)}, bf16[16,512,128]{2,1,0:T(8,128)(2,1)}, u32[]{:S(2)}) copy-start(bf16[16,512,128]{2,1,0:T(8,128)(2,1)} %param.13) | copy-start | bytes 6291460
  4.2 24.6 %all-to-all-start = ((bf16[8,64,576]{2,1,0:T(8,128)(2,1)}), bf16[8,64,576]{2,1,0:T(8,128)(2,1)S(1)}, u32[]{:S(2)}, u32[]{:S(2)}) async-start(bf16[8,64,576]{2,1,0:T(8,128)(2,1)} %reshape.179), calls=%async_computation | async-start | bytes 1310720 | tf_op jit(solution)/shard_map/all_to_all | solution.py:56
  11.5 14.1 %copy-start.5 = (s32[1,1,8]{2,1,0:T(1,128)S(1)}, s32[1,1,8]{2,1,0:T(1,128)}, u32[]{:S(2)}) copy-start(s32[1,1,8]{2,1,0:T(1,128)} %param.11) | copy-start | bytes 100
  34.5 1.3 %copy-start.1 = (f32[8,64,1024]{2,1,0:T(8,128)}, f32[8,64,1024]{2,1,0:T(8,128)S(1)}, u32[]{:S(2)}) copy-start(f32[8,64,1024]{2,1,0:T(8,128)S(1)} %get-tuple-element.10) | copy-start | bytes 6291460
  37.0 10.3 %all-to-all-start.1 = ((f32[8,1,64]{2,1,0:T(1,128)}), f32[8,1,64]{2,1,0:T(1,128)S(1)}, u32[]{:S(2)}, u32[]{:S(2)}) async-start(f32[8,1,64]{2,1,0:T(1,128)} %bitcast.6), calls=%async_computation.1 | async-start | bytes 8192 | tf_op jit(solution)/shard_map/all_to_all | solution.py:61
  47.3 6.1 %copy-start.6 = (s32[4,1]{0,1:T(1,128)S(1)}, s32[4,1]{0,1:T(1,128)}, u32[]{:S(2)}) copy-start(s32[4,1]{0,1:T(1,128)} %param.9) | copy-start | bytes 52
  47.3 6.2 %copy-start.2 = (bf16[4,64,576]{2,1,0:T(8,128)(2,1)S(1)}, bf16[4,64,576]{2,1,0:T(8,128)(2,1)}, u32[]{:S(2)}) copy-start(bf16[4,64,576]{2,1,0:T(8,128)(2,1)} %param.7) | copy-start | bytes 884740
  47.3 8.8 %copy-start.4 = (s32[1,1,8]{2,1,0:T(1,128)S(1)}, s32[1,1,8]{2,1,0:T(1,128)}, u32[]{:S(2)}) copy-start(s32[1,1,8]{2,1,0:T(1,128)} %param.12) | copy-start | bytes 100
  47.3 31.7 %all-to-all-start.3 = ((f32[8,64,512]{2,1,0:T(8,128)}), f32[8,64,512]{2,1,0:T(8,128)S(1)}, u32[]{:S(2)}, u32[]{:S(2)}) async-start(f32[8,64,512]{2,1,0:T(8,128)} %fusion.21), calls=%async_computation.3 | async-start | bytes 2097152 | tf_op jit(solution)/shard_map/all_to_all | solution.py:60
  55.3 0.7 copy-start.3
  79.0 7.9 %all-to-all-start.2 = ((f32[1,4,64]{1,0,2:T(1,128)}), f32[1,4,64]{1,0,2:T(1,128)S(1)}, u32[]{:S(2)}, u32[]{:S(2)}) async-start(f32[1,4,64]{1,0,2:T(1,128)} %copy.35), calls=%async_computation.2 | async-start | bytes 65536 | tf_op jit(solution)/shard_map/all_to_all | solution.py:31
  86.9 12.3 %all-to-all-start.4 = ((f32[1,4,64,512]{3,1,0,2:T(4,128)}), f32[1,4,64,512]{3,1,0,2:T(4,128)S(1)}, u32[]{:S(2)}, u32[]{:S(2)}) async-start(f32[1,4,64,512]{3,1,0,2:T(4,128)} %copy.41), calls=%async_computation.4 | async-start | bytes 1048576 | tf_op jit(solution)/shard_map/all_to_all | solution.py:30
where the time goes:
time: 101 us; the launch traced here: 100 us
  waiting for transfers between devices  33.1 us (33%)
  starting transfers between devices  23.8 us (24%)
  local copies, waits for them, and re-layouts  22.2 us (22%)
  matrix products  18.9 us (19%)
  other arithmetic  2.27 us (2%)
    all_to_all x1, waiting for transfers between devices, local(): lax.all_to_all(helper_out, 'dp', split_axis=0, concat_axis=0, tiled=True)  21.4 us
    unnamed x15, local copies, waits for them, and re-layouts  16.1 us
    all_to_all x1, waiting for transfers between devices, combine_group(): lax.all_to_all(device_out[None], 'sub', split_axis=2, concat_axis=0, tile...  8.63 us
    dot_general x2, matrix products, attend(): jnp.einsum('pht,ptd->phd', weights, slot_cache[:, :, :DL], preferred_elem...  8.5 us
    dot_general x2, matrix products, attend(): jnp.einsum('phd,ptd->pht', queries, slot_cache, preferred_element_type=jn...  7.35 us
    all_to_all x1, starting transfers between devices, local(): lax.all_to_all(outgoing, 'dp', split_axis=0, concat_axis=0, tiled=True)  7.31 us
    all_to_all x1, starting transfers between devices, local(): lax.all_to_all(helper_out, 'dp', split_axis=0, concat_axis=0, tiled=True)  6.13 us
    all_to_all x1, starting transfers between devices, local(): lax.all_to_all(helper_lse, 'dp', split_axis=0, concat_axis=0, tiled=True)  3.64 us
  transfers between devices with their start and end apart: 5, of which 3 were waited for; matrix products, arithmetic and copies ran while one was open for 29% of the time, Pallas kernels for 0%

commit v1 on v0

--- a/solution.py
+++ b/solution.py
@@ -6,6 +6,18 @@
 DL = 512
 score_scale = 192 ** (-0.5)
 masked_score = -1e30
+
+
+def get_signs_now(target, row_dim, x_local):
+    right_arr, prior = (target.shape[:row_dim], target.shape[row_dim + 1 :])
+    placed = target.reshape(*right_arr, x_local, -1, *prior)
+    return jnp.moveaxis(placed, row_dim, 0)
+
+
+def _rest_records(block_here, axis_no):
+    tile_out = list(block_here.shape[1:])
+    tile_out[axis_no] *= block_here.shape[0]
+    return jnp.moveaxis(block_here, 0, axis_no).reshape(tile_out)
 
 
 def attend(queries, slot_cache, lengths):
@@ -58,7 +70,19 @@
         slot_lengths,
     )
     back_out = lax.all_to_all(helper_out, "dp", split_axis=0, concat_axis=0, tiled=True)
-    back_lse = lax.all_to_all(helper_lse, "dp", split_axis=0, concat_axis=0, tiled=True)
+
+    def define_the_figure(vals, mesh_name, z_in, sample):
+        reached, met_up = (lax.psum(1, axis_name=mesh_name), lax.axis_index(mesh_name))
+        k_now = get_signs_now(vals, z_in, reached)
+        xs_all = [k_now[met_up]]
+        for ix in range(1, reached):
+            mixed_arr = k_now[met_up ^ ix]
+            piece_out = lax.ppermute(mixed_arr, mesh_name, [(ii, ii ^ ix) for ii in range(reached)])
+            xs_all.append(piece_out)
+        k_now = jnp.stack(xs_all, axis=0)[met_up ^ jnp.arange(reached)]
+        return _rest_records(k_now, sample)
+
+    back_lse = define_the_figure(helper_lse, "dp", 0, 0)
     own_out, own_lse = attend(queries, own_cache, own_len.reshape(request_count))
     masked = jnp.where(matched[:, :, None], back_lse[:, None, :], masked_score)
     largest = jnp.maximum(own_lse, jnp.max(masked, axis=0))

time: 101 us -> 93 us (0.921)
  waiting for transfers between devices: 33.1 us -> 19.7 us
  starting transfers between devices: 23.8 us -> 33 us
  matrix products: 18.9 us -> 15.5 us
  local copies, waits for them, and re-layouts: 22.2 us -> 21 us
    all_to_all x1, waiting for transfers between devices: 21.4 us -> 0.01 us  [local(): lax.all_to_all(helper_out, 'dp', split_axis=0, concat_axis=0, tiled=True)]
    ppermute x0 -> x7, starting transfers between devices: none -> 15.2 us  [define_the_figure(): lax.ppermute(mixed_arr, mesh_name, [(ii, ii ^ ix) for ii in range(reached)])]
    ppermute x0 -> x7, waiting for transfers between devices: none -> 8.05 us  [define_the_figure(): lax.ppermute(mixed_arr, mesh_name, [(ii, ii ^ ix) for ii in range(reached)])]
    dot_general x2, matrix products: 8.5 us -> 4.27 us  [attend(): jnp.einsum('pht,ptd->phd', weights, slot_cache[:, :, :DL], preferred_elem...]
    all_to_all x1 -> x0, starting transfers between devices: 3.64 us -> none  [local(): lax.all_to_all(helper_lse, 'dp', split_axis=0, concat_axis=0, tiled=True)]
    all_to_all x1, starting transfers between devices: 6.13 us -> 3.77 us  [local(): lax.all_to_all(helper_out, 'dp', split_axis=0, concat_axis=0, tiled=True)]
    unnamed x15, local copies, waits for them, and re-layouts: 16.1 us -> 14.3 us
    reduce_sum x2, other arithmetic: 0.78 us -> 1.82 us  [attend(): totals = jnp.sum(exponent, axis=2)]
  transfers between devices with their start and end apart: 5 -> 11, of which waited for: 3 -> 5; matrix products, arithmetic and copies ran while one was open for 29% -> 27% of each run, Pallas kernels for 0% -> 0%
where the time goes in v1:
time: 93 us; the launch traced here: 92.1 us
  starting transfers between devices  33 us (35%)
  local copies, waits for them, and re-layouts  21 us (23%)
  waiting for transfers between devices  19.7 us (21%)
  matrix products  15.5 us (17%)
  other arithmetic  2.72 us (3%)
    ppermute x7, starting transfers between devices, define_the_figure(): lax.ppermute(mixed_arr, mesh_name, [(ii, ii ^ ix) for ii in range(reached)])  15.2 us
    unnamed x15, local copies, waits for them, and re-layouts  14.3 us
    all_to_all x1, waiting for transfers between devices, combine_group(): lax.all_to_all(device_out[None], 'sub', split_axis=2, concat_axis=0, tile...  8.63 us
    dot_general x2, matrix products, attend(): jnp.einsum('phd,ptd->pht', queries, slot_cache, preferred_element_type=jn...  8.13 us
    ppermute x7, waiting for transfers between devices, define_the_figure(): lax.ppermute(mixed_arr, mesh_name, [(ii, ii ^ ix) for ii in range(reached)])  8.05 us
    all_to_all x1, starting transfers between devices, local(): lax.all_to_all(outgoing, 'dp', split_axis=0, concat_axis=0, tiled=True)  7.31 us
    dot_general x2, matrix products, attend(): jnp.einsum('pht,ptd->phd', weights, slot_cache[:, :, :DL], preferred_elem...  4.27 us
    all_to_all x1, starting transfers between devices, local(): lax.all_to_all(helper_out, 'dp', split_axis=0, concat_axis=0, tiled=True)  3.77 us
  transfers between devices with their start and end apart: 11, of which 5 were waited for; matrix products, arithmetic and copies ran while one was open for 27% of the time, Pallas kernels for 0%

profile of v1, /device:TPU:0, one launch (start us, length us, event | category | flops | bytes accessed | tf_op | source)
XLA Modules:
  0.0 92.1 jit_solution(2957919704929497258)
XLA Ops:
  0.0 1.5 %reshape.190 = bf16[4,36864]{1,0:T(4,128)(2,1)S(1)} reshape(bf16[4,64,576]{2,1,0:T(8,128)(2,1)} %param.7) | data formatting | bytes 589824 | tf_op jit(solution)/shard_map/reshape | solution.py:61
  1.5 1.0 %convolution_convert_fusion = bf16[8,36864]{1,0:T(8,128)(2,1)S(1)} fusion(bf16[4,36864]{1,0:T(4,128)(2,1)S(1)} %reshape.190, s32[8]{0:T(128)} %bitcast.87), kind=kOutput, calls=%fused_computation.1 | convolution fusion | flops 2654240 | bytes 884768 | tf_op jit(solution)/shard_map/dot_general | solution.py:59
  2.6 1.7 %reshape.191 = bf16[8,64,576]{2,1,0:T(8,128)(2,1)} reshape(bf16[8,36864]{1,0:T(8,128)(2,1)S(1)} %convolution_convert_fusion) | data formatting | bytes 1179648 | tf_op jit(solution)/shard_map/reshape | solution.py:64
  4.2 7.3 %all-to-all-start = ((bf16[8,64,576]{2,1,0:T(8,128)(2,1)}), bf16[8,64,576]{2,1,0:T(8,128)(2,1)S(1)}, u32[]{:S(2)}, u32[]{:S(2)}) async-start(bf16[8,64,576]{2,1,0:T(8,128)(2,1)} %reshape.191), calls=%async_computation | async-start | bytes 1310720 | tf_op jit(solution)/shard_map/all_to_all | solution.py:68
  11.5 0.0 copy-start.5
  11.5 14.1 %copy.44 = bf16[1,1,8,1024,576]{4,3,2,1,0:T(8,128)(2,1)} copy(bf16[1,1,8,1024,576]{3,4,2,1,0:T(8,128)(2,1)} %param.10) | data formatting | bytes 18874368 | tf_op args[3]
  25.6 0.1 iota_compare_fusion.1
  25.7 0.1 iota_compare_fusion
  25.8 3.0 %all-to-all-done = bf16[8,64,576]{2,1,0:T(8,128)(2,1)S(1)} async-done(((bf16[8,64,576]{2,1,0:T(8,128)(2,1)}), bf16[8,64,576]{2,1,0:T(8,128)(2,1)S(1)}, u32[]{:S(2)}, u32[]{:S(2)}) %all-to-all-start) | async-done | bytes 589856 | tf_op jit(solution)/shard_map/all_to_all | solution.py:68
  28.8 5.8 %fusion.4 = (f32[8,64]{1,0:T(8,128)S(1)}, f32[8,64,1024]{2,1,0:T(8,128)S(1)}) fusion(pred[8,1024]{1,0:T(8,128)(4,1)S(1)} %iota_compare_fusion, bf16[8,64,576]{2,1,0:T(8,128)(2,1)S(1)} %all-to-all-done, bf16[1,1,8,1024,576]{3,4,2,1,0:T(8,128)(2,1)} %param.10), kind=kOutput, calls=%fused_computation.8 | convolution fusion | flops 605552128 | bytes 12134400 | tf_op jit(solution)/shard_map/phd,ptd->pht/dot_general | solution.py:25
  34.6 0.6 fusion.6
  35.3 0.2 copy-done.1
  35.5 2.5 %fusion.21 = f32[8,64,512]{2,1,0:T(8,128)} fusion(bf16[8,1024,576]{2,1,0:T(8,128)(2,1)S(1)} %bitcast.83, f32[8,64,1024]{2,1,0:T(8,128)S(1)} %get-tuple-element.18, f32[8,64]{1,0:T(8,128)S(1)} %get-tuple-element.17, pred[8,1024]{1,0:T(8,128)(4,1)S(1)} %iota_compare_fusion, f32[8,64]{1,0:T(8,128)S(1)} %fusion.6), kind=kOutput, calls=%fused_computation.27 | convolution fusion | flops 539230208 | bytes 11550720 | tf_op jit(solution)/shard_map/pht,ptd->phd/dot_general | solution.py:34
  38.0 3.8 %all-to-all-start.2 = ((f32[8,64,512]{2,1,0:T(8,128)}), f32[8,64,512]{2,1,0:T(8,128)S(1)}, u32[]{:S(2)}, u32[]{:S(2)}) async-start(f32[8,64,512]{2,1,0:T(8,128)} %fusion.21), calls=%async_computation.2 | async-start | bytes 2097152 | tf_op jit(solution)/shard_map/all_to_all | solution.py:72
  41.8 2.3 %fusion.52 = (f32[4,64]{1,0:T(4,128)S(1)}, f32[4,64,256]{2,1,0:T(8,128)}) fusion(bf16[4,64,576]{2,1,0:T(8,128)(2,1)S(1)} %copy-done.2, bf16[4,256,576]{1,2,0:T(8,128)(2,1)} %param.8, pred[4,256]{1,0:T(4,128)(4,1)S(1)} %iota_compare_fusion.1), kind=kOutput, calls=%fused_computation.77 | convolution fusion | flops 75693824 | bytes 1738752 | tf_op jit(solution)/shard_map/phd,ptd->pht/dot_general | solution.py:25
  44.2 1.2 %fusion.28 = f32[4,64]{1,0:T(4,128)S(1)} fusion(f32[4,64,256]{2,1,0:T(8,128)} %get-tuple-element.20, f32[4,64]{1,0:T(4,128)S(1)} %get-tuple-element.19), kind=kLoop, calls=%fused_computation.32 | loop fusion | flops 130816 | bytes 264192 | tf_op jit(solution)/shard_map/reduce_sum | solution.py:32
  45.4 2.1 %collective-permute-start = (f32[1,64]{1,0:T(1,128)S(1)}, f32[1,64]{1,0:T(1,128)S(1)}, u32[]{:S(2)}, u32[]{:S(2)}) collective-permute-start(f32[1,64]{1,0:T(1,128)S(1)} %get-tuple-element.15), channel_id=1, source_target_pairs={{0,4},{4,0},{8,12},{12,8},{16,20},{20,16},{24,28},{28,24},{1,5},{5... | collective-permute-start | bytes 776 | tf_op jit(solution)/shard_map/ppermute | solution.py:80
  47.5 1.5 %collective-permute-start.1 = (f32[1,64]{1,0:T(1,128)S(1)}, f32[1,64]{1,0:T(1,128)S(1)}, u32[]{:S(2)}, u32[]{:S(2)}) collective-permute-start(f32[1,64]{1,0:T(1,128)S(1)} %get-tuple-element.14), channel_id=1, source_target_pairs={{0,8},{4,12},{8,0},{12,4},{16,24},{20,28},{24,16},{28,20},{1,9},{5... | collective-permute-start | bytes 776 | tf_op jit(solution)/shard_map/ppermute | solution.py:80
  49.0 0.1 collective-permute-start.2
  49.1 2.8 %collective-permute-start.3 = (f32[1,64]{1,0:T(1,128)S(1)}, f32[1,64]{1,0:T(1,128)S(1)}, u32[]{:S(2)}, u32[]{:S(2)}) collective-permute-start(f32[1,64]{1,0:T(1,128)S(1)} %get-tuple-element.12), channel_id=1, source_target_pairs={{0,16},{4,20},{8,24},{12,28},{16,0},{20,4},{24,8},{28,12},{1,17},{... | collective-permute-start | bytes 776 | tf_op jit(solution)/shard_map/ppermute | solution.py:80
  51.9 1.5 %collective-permute-start.4 = (f32[1,64]{1,0:T(1,128)S(1)}, f32[1,64]{1,0:T(1,128)S(1)}, u32[]{:S(2)}, u32[]{:S(2)}) collective-permute-start(f32[1,64]{1,0:T(1,128)S(1)} %get-tuple-element.11), channel_id=1, source_target_pairs={{0,20},{4,16},{8,28},{12,24},{16,4},{20,0},{24,12},{28,8},{1,21},{... | collective-permute-start | bytes 776 | tf_op jit(solution)/shard_map/ppermute | solution.py:80
  53.4 0.0 collective-permute-done
  53.4 3.3 %collective-permute-start.5 = (f32[1,64]{1,0:T(1,128)S(1)}, f32[1,64]{1,0:T(1,128)S(1)}, u32[]{:S(2)}, u32[]{:S(2)}) collective-permute-start(f32[1,64]{1,0:T(1,128)S(1)} %get-tuple-element.10), channel_id=1, source_target_pairs={{0,24},{4,28},{8,16},{12,20},{16,8},{20,12},{24,0},{28,4},{1,25},{... | collective-permute-start | bytes 776 | tf_op jit(solution)/shard_map/ppermute | solution.py:80
  56.6 3.0 %collective-permute-done.1 = f32[1,64]{1,0:T(1,128)S(1)} collective-permute-done((f32[1,64]{1,0:T(1,128)S(1)}, f32[1,64]{1,0:T(1,128)S(1)}, u32[]{:S(2)}, u32[]{:S(2)}) %collective-permute-start.1) | collective-permute-done | bytes 288 | tf_op jit(solution)/shard_map/ppermute | solution.py:80
  59.6 4.0 %collective-permute-start.6 = (f32[1,64]{1,0:T(1,128)S(1)}, f32[1,64]{1,0:T(1,128)S(1)}, u32[]{:S(2)}, u32[]{:S(2)}) collective-permute-start(f32[1,64]{1,0:T(1,128)S(1)} %get-tuple-element.9), channel_id=1, source_target_pairs={{0,28},{4,24},{8,20},{12,16},{16,12},{20,8},{24,4},{28,0},{1,29},{... | collective-permute-start | bytes 776 | tf_op jit(solution)/shard_map/ppermute | solution.py:80
  63.6 4.3 %collective-permute-done.3 = f32[1,64]{1,0:T(1,128)S(1)} collective-permute-done((f32[1,64]{1,0:T(1,128)S(1)}, f32[1,64]{1,0:T(1,128)S(1)}, u32[]{:S(2)}, u32[]{:S(2)}) %collective-permute-start.3) | collective-permute-done | bytes 288 | tf_op jit(solution)/shard_map/ppermute | solution.py:80
  67.9 0.8 collective-permute-done.4
  68.7 0.0 collective-permute-done.5
  68.7 0.0 collective-permute-done.6
  68.7 0.6 gather_fusion
  69.3 0.1 copy.54
  69.4 0.1 select_reduce_fusion
  69.5 0.1 copy.55
  69.6 0.1 copy.57
  69.7 0.2 fusion.31
  69.9 0.1 copy.58
  70.0 0.7 copy.59
  70.8 3.3 %all-to-all-start.1 = ((f32[1,4,64]{1,0,2:T(1,128)}), f32[1,4,64]{1,0,2:T(1,128)S(1)}, u32[]{:S(2)}, u32[]{:S(2)}) async-start(f32[1,4,64]{1,0,2:T(1,128)} %copy.59), calls=%async_computation.1 | async-start | bytes 65536 | tf_op jit(solution)/shard_map/all_to_all | solution.py:43
  74.1 1.6 %fusion.14 = f32[64,512,4]{1,2,0:T(4,128)S(1)} fusion(f32[8,64,512]{2,1,0:T(8,128)S(1)} %all-to-all-done.2, f32[8,64]{0,1:T(8,128)S(1)} %copy.54, f32[4,64]{0,1:T(8,128)S(1)} %copy.57, pred[8,4]{0,1:T(4,128)(4,1)S(1)} %iota_compare_fusion.2), kind=kOutput, calls=%fused_computation.20 | convolution fusion | flops 12587008 | bytes 1575968 | tf_op jit(solution)/shard_map/pch,phd->chd/dot_general | solution.py:91
  75.7 1.7 %fusion.10 = f32[1,4,64,512]{3,2,1,0:T(8,128)S(1)} fusion(bf16[4,256,576]{1,2,0:T(8,128)(2,1)} %param.8, f32[64,512,4]{1,2,0:T(4,128)S(1)} %fusion.14, f32[4,64]{1,0:T(4,128)S(1)} %get-tuple-element.7, f32[4,64]{1,0:T(4,128)S(1)} %fusion.28, f32[4,64]{1,0:T(4,128)S(1)} %get-tuple-element.8, f32[4,64,256]{2,1,0:T(8,128)S(1)} %copy-done.3, ...), kind=kOutput, calls=%fused_computation.15 | convolution fusion | flops 67764224 | bytes 2363392 | tf_op jit(solution)/shard_map/pht,ptd->phd/dot_general | solution.py:34
  77.5 1.1 %copy.65 = f32[1,4,64,512]{3,1,0,2:T(4,128)} copy(f32[1,4,64,512]{3,2,1,0:T(8,128)S(1)} %fusion.10) | data formatting | bytes 1048576 | tf_op jit(solution)/shard_map/broadcast_in_dim | solution.py:42
  78.6 3.5 %all-to-all-start.3 = ((f32[1,4,64,512]{3,1,0,2:T(4,128)}), f32[1,4,64,512]{3,1,0,2:T(4,128)S(1)}, u32[]{:S(2)}, u32[]{:S(2)}) async-start(f32[1,4,64,512]{3,1,0,2:T(4,128)} %copy.65), calls=%async_computation.3 | async-start | bytes 1048576 | tf_op jit(solution)/shard_map/all_to_all | solution.py:42
  82.1 0.1 copy.60
  82.2 8.6 %all-to-all-done.3 = f32[1,4,64,512]{3,1,0,2:T(4,128)S(1)} async-done(((f32[1,4,64,512]{3,1,0,2:T(4,128)}), f32[1,4,64,512]{3,1,0,2:T(4,128)S(1)}, u32[]{:S(2)}, u32[]{:S(2)}) %all-to-all-start.3) | async-done | bytes 524320 | tf_op jit(solution)/shard_map/all_to_all | solution.py:42
  90.8 0.2 fusion.26
  91.0 0.1 divide_convert_fusion
  91.1 0.4 fusion.12
  91.5 0.6 copy.68
  (26 shorter events, 0.2 us)
Async XLA Ops:
  0.0 91.1 %copy-start = (bf16[16,512,128]{2,1,0:T(8,128)(2,1)S(1)}, bf16[16,512,128]{2,1,0:T(8,128)(2,1)}, u32[]{:S(2)}) copy-start(bf16[16,512,128]{2,1,0:T(8,128)(2,1)} %param.13) | copy-start | bytes 6291460
  4.2 24.6 %all-to-all-start = ((bf16[8,64,576]{2,1,0:T(8,128)(2,1)}), bf16[8,64,576]{2,1,0:T(8,128)(2,1)S(1)}, u32[]{:S(2)}, u32[]{:S(2)}) async-start(bf16[8,64,576]{2,1,0:T(8,128)(2,1)} %reshape.191), calls=%async_computation | async-start | bytes 1310720 | tf_op jit(solution)/shard_map/all_to_all | solution.py:68
  11.5 14.1 %copy-start.6 = (s32[4,1]{0,1:T(1,128)S(1)}, s32[4,1]{0,1:T(1,128)}, u32[]{:S(2)}) copy-start(s32[4,1]{0,1:T(1,128)} %param.9) | copy-start | bytes 52
  11.5 14.2 %copy-start.5 = (s32[1,1,8]{2,1,0:T(1,128)S(1)}, s32[1,1,8]{2,1,0:T(1,128)}, u32[]{:S(2)}) copy-start(s32[1,1,8]{2,1,0:T(1,128)} %param.11) | copy-start | bytes 100
  28.8 6.7 %copy-start.1 = (bf16[1,1,8,1024,576]{4,3,2,1,0:T(8,128)(2,1)S(1)}, bf16[1,1,8,1024,576]{4,3,2,1,0:T(8,128)(2,1)}, u32[]{:S(2)}) copy-start(bf16[1,1,8,1024,576]{4,3,2,1,0:T(8,128)(2,1)} %copy.44) | copy-start | bytes 28311556
  38.0 3.8 %copy-start.2 = (bf16[4,64,576]{2,1,0:T(8,128)(2,1)S(1)}, bf16[4,64,576]{2,1,0:T(8,128)(2,1)}, u32[]{:S(2)}) copy-start(bf16[4,64,576]{2,1,0:T(8,128)(2,1)} %param.7) | copy-start | bytes 884740
  38.0 7.3 %copy-start.4 = (s32[1,1,8]{2,1,0:T(1,128)S(1)}, s32[1,1,8]{2,1,0:T(1,128)}, u32[]{:S(2)}) copy-start(s32[1,1,8]{2,1,0:T(1,128)} %param.12) | copy-start | bytes 100
  38.0 32.7 %all-to-all-start.2 = ((f32[8,64,512]{2,1,0:T(8,128)}), f32[8,64,512]{2,1,0:T(8,128)S(1)}, u32[]{:S(2)}, u32[]{:S(2)}) async-start(f32[8,64,512]{2,1,0:T(8,128)} %fusion.21), calls=%async_computation.2 | async-start | bytes 2097152 | tf_op jit(solution)/shard_map/all_to_all | solution.py:72
  44.2 31.6 %copy-start.3 = (f32[4,64,256]{2,1,0:T(8,128)S(1)}, f32[4,64,256]{2,1,0:T(8,128)}, u32[]{:S(2)}) copy-start(f32[4,64,256]{2,1,0:T(8,128)} %get-tuple-element.20) | copy-start | bytes 786436
  45.4 7.9 %collective-permute-start = (f32[1,64]{1,0:T(1,128)S(1)}, f32[1,64]{1,0:T(1,128)S(1)}, u32[]{:S(2)}, u32[]{:S(2)}) collective-permute-start(f32[1,64]{1,0:T(1,128)S(1)} %get-tuple-element.15), channel_id=1, source_target_pairs={{0,4},{4,0},{8,12},{12,8},{16,20},{20,16},{24,28},{28,24},{1,5},{5... | collective-permute-start | bytes 776 | tf_op jit(solution)/shard_map/ppermute | solution.py:80
  47.5 12.1 %collective-permute-start.1 = (f32[1,64]{1,0:T(1,128)S(1)}, f32[1,64]{1,0:T(1,128)S(1)}, u32[]{:S(2)}, u32[]{:S(2)}) collective-permute-start(f32[1,64]{1,0:T(1,128)S(1)} %get-tuple-element.14), channel_id=1, source_target_pairs={{0,8},{4,12},{8,0},{12,4},{16,24},{20,28},{24,16},{28,20},{1,9},{5... | collective-permute-start | bytes 776 | tf_op jit(solution)/shard_map/ppermute | solution.py:80
  49.0 14.7 %collective-permute-start.2 = (f32[1,64]{1,0:T(1,128)S(1)}, f32[1,64]{1,0:T(1,128)S(1)}, u32[]{:S(2)}, u32[]{:S(2)}) collective-permute-start(f32[1,64]{1,0:T(1,128)S(1)} %get-tuple-element.13), channel_id=1, source_target_pairs={{0,12},{4,8},{8,4},{12,0},{16,28},{20,24},{24,20},{28,16},{1,13},{... | collective-permute-start | bytes 776 | tf_op jit(solution)/shard_map/ppermute | solution.py:80
  49.1 18.9 %collective-permute-start.3 = (f32[1,64]{1,0:T(1,128)S(1)}, f32[1,64]{1,0:T(1,128)S(1)}, u32[]{:S(2)}, u32[]{:S(2)}) collective-permute-start(f32[1,64]{1,0:T(1,128)S(1)} %get-tuple-element.12), channel_id=1, source_target_pairs={{0,16},{4,20},{8,24},{12,28},{16,0},{20,4},{24,8},{28,12},{1,17},{... | collective-permute-start | bytes 776 | tf_op jit(solution)/shard_map/ppermute | solution.py:80
  51.9 16.8 %collective-permute-start.4 = (f32[1,64]{1,0:T(1,128)S(1)}, f32[1,64]{1,0:T(1,128)S(1)}, u32[]{:S(2)}, u32[]{:S(2)}) collective-permute-start(f32[1,64]{1,0:T(1,128)S(1)} %get-tuple-element.11), channel_id=1, source_target_pairs={{0,20},{4,16},{8,28},{12,24},{16,4},{20,0},{24,12},{28,8},{1,21},{... | collective-permute-start | bytes 776 | tf_op jit(solution)/shard_map/ppermute | solution.py:80
  53.4 15.3 %collective-permute-start.5 = (f32[1,64]{1,0:T(1,128)S(1)}, f32[1,64]{1,0:T(1,128)S(1)}, u32[]{:S(2)}, u32[]{:S(2)}) collective-permute-start(f32[1,64]{1,0:T(1,128)S(1)} %get-tuple-element.10), channel_id=1, source_target_pairs={{0,24},{4,28},{8,16},{12,20},{16,8},{20,12},{24,0},{28,4},{1,25},{... | collective-permute-start | bytes 776 | tf_op jit(solution)/shard_map/ppermute | solution.py:80
  59.6 9.1 %collective-permute-start.6 = (f32[1,64]{1,0:T(1,128)S(1)}, f32[1,64]{1,0:T(1,128)S(1)}, u32[]{:S(2)}, u32[]{:S(2)}) collective-permute-start(f32[1,64]{1,0:T(1,128)S(1)} %get-tuple-element.9), channel_id=1, source_target_pairs={{0,28},{4,24},{8,20},{12,16},{16,12},{20,8},{24,4},{28,0},{1,29},{... | collective-permute-start | bytes 776 | tf_op jit(solution)/shard_map/ppermute | solution.py:80
  70.8 7.8 %all-to-all-start.1 = ((f32[1,4,64]{1,0,2:T(1,128)}), f32[1,4,64]{1,0,2:T(1,128)S(1)}, u32[]{:S(2)}, u32[]{:S(2)}) async-start(f32[1,4,64]{1,0,2:T(1,128)} %copy.59), calls=%async_computation.1 | async-start | bytes 65536 | tf_op jit(solution)/shard_map/all_to_all | solution.py:43
  78.6 12.3 %all-to-all-start.3 = ((f32[1,4,64,512]{3,1,0,2:T(4,128)}), f32[1,4,64,512]{3,1,0,2:T(4,128)S(1)}, u32[]{:S(2)}, u32[]{:S(2)}) async-start(f32[1,4,64,512]{3,1,0,2:T(4,128)} %copy.65), calls=%async_computation.3 | async-start | bytes 1048576 | tf_op jit(solution)/shard_map/all_to_all | solution.py:42
